TPU v7x, 256 devices: a whole 4x4x8 slice. The times are simulated.
256 devices in a mesh: seq: 32 (over x, y, core), head: 8 (over z).
Axes of the slice: x: 4, y: 4, z: 8, core: 2. Of those that a mesh axis runs over, the one named last changes fastest.
Arguments:
- queries: bfloat16 [32768, 64, 128], P(('seq', 'head')), may hold values from -8 to 8
- keys: bfloat16 [32768, 8, 128], P(('seq', 'head')), may hold values from -8 to 8
- values: bfloat16 [32768, 8, 128], P(('seq', 'head')), may hold values from -6 to 6
- ancestors: int32 [256, 8], P('seq'), may hold values from 0 to 255, as said below
- lengths: int32 [256], replicated, may hold values from 2 to 128
Outputs:
- attended: bfloat16 [32768, 64, 128], P(('seq', 'head'))
Inputs may be any that keep to these rules, and one draw needn't show every extreme that they name: The 8 ancestors of a block are distinct blocks held on other indices of seq; the blocks of one index of seq name, all together, exactly 2 distinct blocks of each of 6 other indices and no other block.
All inputs are finite; a program needn't handle non-finite values.
Results may differ from a plain program's by a relative error of at most 0.0049.
Values may be sent and summed in bfloat16 or wider, within the bound.
No kernel may reach another device: no remote copies, remote signals or barrier semaphores. Data moves between devices by JAX's collectives and lax.ppermute only.
A program may use at most 64 MiB of HBM per device.

v0:
```python
import math
import jax
import jax.numpy as jnp
from jax import lax
from jax.sharding import PartitionSpec as P

BS = 128
negative_fill = -1e30


def attend_block(query_block, key_self, value_self, key_far, value_far, length_self, length_far):
    width = query_block.shape[-1]
    block_rows = key_self.shape[0]
    kv_groups = key_self.shape[1]
    far_count = key_far.shape[0]
    key_all = jnp.concatenate([key_self[None], key_far], axis=0).reshape(-1, kv_groups, width)
    value_all = jnp.concatenate([value_self[None], value_far], axis=0).reshape(-1, kv_groups, width)
    scores = jnp.einsum("tgsd,kgd->gstk", query_block, key_all, preferred_element_type=jnp.float32)
    scores = scores * (1.0 / math.sqrt(width))
    offsets_row = jnp.arange(block_rows, dtype=jnp.int32)
    self_mask = (offsets_row[None, :] <= offsets_row[:, None]) & (
        offsets_row[None, :] < length_self
    )
    far_mask = (offsets_row[None, :] < length_far[:, None]).reshape(1, far_count * block_rows)
    far_mask = jnp.broadcast_to(far_mask, (block_rows, far_count * block_rows))
    allowed = jnp.concatenate([self_mask, far_mask], axis=1)
    scores = jnp.where(allowed, scores, negative_fill)
    largest = jnp.max(scores, axis=-1, keepdims=True)
    exponent = jnp.exp(scores - largest)
    weights = (exponent / jnp.sum(exponent, axis=-1, keepdims=True)).astype(jnp.bfloat16)
    mixed = jnp.einsum("gstk,kgd->tgsd", weights, value_all, preferred_element_type=jnp.float32)
    return mixed.astype(jnp.bfloat16)


def attend_items(items):
    query_block, key_self, value_self, key_far, value_far, length_self, length_far = items
    return attend_block(
        query_block, key_self, value_self, key_far, value_far, length_self, length_far
    )


def local(queries, keys, values, ancestors, lengths):
    query_local, key_local, value_local = (
        lax.all_to_all(queries, "head", split_axis=1, concat_axis=0, tiled=True),
        lax.all_to_all(keys, "head", split_axis=1, concat_axis=0, tiled=True),
        lax.all_to_all(values, "head", split_axis=1, concat_axis=0, tiled=True),
    )
    token_rows, head_count, width = query_local.shape
    kv_groups = key_local.shape[1]
    blk_dev = token_rows // BS
    seq_place = lax.axis_index("seq")
    key_blocks = key_local.reshape(blk_dev, BS, kv_groups, width)
    value_blocks = value_local.reshape(blk_dev, BS, kv_groups, width)
    key_every, value_every = (
        lax.all_gather(key_local, "seq", axis=0, tiled=True),
        lax.all_gather(value_local, "seq", axis=0, tiled=True),
    )
    key_every = key_every.reshape(-1, BS, kv_groups, width)
    value_every = value_every.reshape(-1, BS, kv_groups, width)
    key_far = jnp.take(key_every, ancestors, axis=0)
    value_far = jnp.take(value_every, ancestors, axis=0)
    length_self = lax.dynamic_slice_in_dim(lengths, seq_place * blk_dev, blk_dev)
    length_far = jnp.take(lengths, ancestors, axis=0)
    query_blocks = query_local.reshape(blk_dev, BS, kv_groups, head_count // kv_groups, width)
    mixed = lax.map(
        attend_items,
        (query_blocks, key_blocks, value_blocks, key_far, value_far, length_self, length_far),
    )
    mixed = mixed.reshape(token_rows, head_count, width)
    return lax.all_to_all(mixed, "head", split_axis=0, concat_axis=1, tiled=True)


def solution(mesh):
    placed = (
        P(("seq", "head"), None, None),
        P(("seq", "head"), None, None),
        P(("seq", "head"), None, None),
        P("seq", None),
        P(),
    )
    return jax.shard_map(
        local, mesh=mesh, in_specs=placed, out_specs=P(("seq", "head"), None, None), check_vma=False
    )
```

profile of v0, /device:TPU:1, one launch (start us, length us, event | category | flops | bytes accessed | tf_op | source)
XLA Modules:
  0.0 284.1 jit_solution(3996163437452136307)
XLA Ops:
  7.7 19.4 %all_to_all.69 = bf16[128,8,128]{2,0,1:T(8,128)(2,1)} all-to-all(bf16[128,8,128]{2,0,1:T(8,128)(2,1)S(1)} %copy.28), channel_id=1, replica_groups=mesh['seq'=32,'head'=8] {'head'}, dimensions={1} | all-to-all | bytes 524288 | tf_op jit(solution)/shard_map/all_to_all | solution.py:45
  28.1 12.5 %all_to_all.70 = bf16[128,8,128]{2,0,1:T(8,128)(2,1)} all-to-all(bf16[128,8,128]{2,0,1:T(8,128)(2,1)S(1)} %copy.27), channel_id=1, replica_groups=mesh['seq'=32,'head'=8] {'head'}, dimensions={1} | all-to-all | bytes 524288 | tf_op jit(solution)/shard_map/all_to_all | solution.py:46
  40.7 2.7 copy.29
  43.4 4.5 %all-to-all-start.2 = ((bf16[128,64,128]{2,0,1:T(8,128)(2,1)}), bf16[128,64,128]{2,0,1:T(8,128)(2,1)}, u32[]{:S(2)}, u32[]{:S(2)}) async-start(bf16[128,64,128]{2,0,1:T(8,128)(2,1)} %copy.29), calls=%async_computation.2 | async-start | bytes 4194304 | tf_op jit(solution)/shard_map/all_to_all | solution.py:44
  48.9 34.5 %all-gather.5.cloned.1.call-done = bf16[32768,1,128]{2,0,1:T(8,128)(2,1)} async-done(((bf16[1024,1,128]{2,0,1:T(8,128)(2,1)}), bf16[32768,1,128]{2,0,1:T(8,128)(2,1)}) %all-gather.5.cloned.1.call-update) | async-done | bytes 8388624 | tf_op jit(solution)/shard_map/all_gather | solution.py:55
  83.5 4.3 %gather_fusion.2 = bf16[64,128,128]{2,1,0:T(8,128)(2,1)S(1)} fusion(bf16[256,128,128]{2,1,0:T(8,128)(2,1)} %bitcast.124, s32[1024]{0:T(1024)S(1)} %pad_clamp_fusion), kind=kCustom, calls=%fused_computation.1.clone | custom fusion | bytes 4194560 | tf_op jit(solution)/shard_map/jit(_take)/gather | solution.py:60
  87.8 55.7 %all-gather.3.cloned.1.call-done = bf16[32768,1,128]{2,0,1:T(8,128)(2,1)} async-done(((bf16[1024,1,128]{2,0,1:T(8,128)(2,1)}), bf16[32768,1,128]{2,0,1:T(8,128)(2,1)}) %all-gather.3.cloned.1.call-update) | async-done | bytes 8388624 | tf_op jit(solution)/shard_map/all_gather | solution.py:56
  143.5 5.6 %gather_fusion.1 = bf16[64,128,128]{2,1,0:T(8,128)(2,1)} fusion(bf16[256,128,128]{2,1,0:T(8,128)(2,1)} %bitcast.125, s32[1024]{0:T(1024)S(1)} %pad_clamp_fusion), kind=kCustom, calls=%fused_computation.clone | custom fusion | bytes 4194560 | tf_op jit(solution)/shard_map/jit(_take)/gather | solution.py:61
  149.1 1.6 broadcast_select_fusion
  151.7 65.8 %while.10 = (s32[]{:T(128)}, bf16[8,128,1,8,128]{4,3,1,0,2:T(8,128)(2,1)}, bf16[8,128,1,128]{3,1,0,2:T(8,128)(2,1)}, bf16[8,8,128,1,128]{4,2,1,3,0:T(8,128)(2,1)...) while((s32[]{:T(128)}, ...), condition=%wide.region_3.5_spmd, body=%wide.region_0.4_spmd.sunk | while | flops 616381568 | bytes 19325688 | solution.py:65
  155.1 1.8 fusion.34
  157.8 1.3 fusion.36
  163.4 1.8 fusion.34
  166.0 1.3 fusion.36
  171.6 1.8 fusion.34
  174.2 1.3 fusion.36
  179.8 1.8 fusion.34
  182.4 1.3 fusion.36
  188.1 1.8 fusion.34
  196.3 1.8 fusion.34
  204.5 1.8 fusion.34
  212.7 1.8 fusion.34
  217.5 57.8 %all_to_all.71 = bf16[1024,8,128]{2,1,0:T(8,128)(2,1)S(1)} all-to-all(bf16[1024,8,128]{2,1,0:T(8,128)(2,1)} %bitcast.119), channel_id=1, replica_groups=mesh['seq'=32,'head'=8] {'head'}, dimensions={0} | all-to-all | bytes 4194304 | tf_op jit(solution)/shard_map/all_to_all | solution.py:70
  275.3 1.9 copy.39
  (140 shorter events, 50.3 us)
Async XLA Ops:
  6.5 34.1 %copy-start.2 = (bf16[128,64,128]{2,1,0:T(8,128)(2,1)S(1)}, bf16[128,64,128]{2,1,0:T(8,128)(2,1)}, u32[]{:S(2)}) copy-start(bf16[128,64,128]{2,1,0:T(8,128)(2,1)} %param.9) | copy-start | bytes 6291460
  6.5 76.9 %all-gather.5.cloned.1.call-start = ((), (), s32[]{:S(2)}) async-start(), calls=%async_computation.5 | async-start | bytes 8650752 | tf_op jit(solution)/shard_map/all_gather | solution.py:55
  27.1 116.4 %all-gather.3.cloned.1.call-start = ((), (), s32[]{:S(2)}) async-start(), calls=%async_computation.4 | async-start | bytes 8650752 | tf_op jit(solution)/shard_map/all_gather | solution.py:56
  43.4 4.5 %copy-start.3 = (s32[8,8]{1,0:T(8,128)S(1)}, s32[8,8]{1,0:T(8,128)}, u32[]{:S(2)}) copy-start(s32[8,8]{1,0:T(8,128)} %param.12) | copy-start | bytes 772
  43.4 4.6 %copy-start = (s32[256]{0:T(256)S(1)}, s32[256]{0:T(256)}, u32[]{:S(2)}) copy-start(s32[256]{0:T(256)} %param.13) | copy-start | bytes 3076
  43.4 108.3 %all-to-all-start.2 = ((bf16[128,64,128]{2,0,1:T(8,128)(2,1)}), bf16[128,64,128]{2,0,1:T(8,128)(2,1)}, u32[]{:S(2)}, u32[]{:S(2)}) async-start(bf16[128,64,128]{2,0,1:T(8,128)(2,1)} %copy.29), calls=%async_computation.2 | async-start | bytes 4194304 | tf_op jit(solution)/shard_map/all_to_all | solution.py:44
  149.1 2.3 copy-start.1
Sparse Core Ops, SparseCore 0:
  27.2 56.1 all-gather.4
  86.0 57.4 all-gather.2
where the time goes:
time: 286 us; the launch traced here: 284 us
  waiting for transfers between devices  90.2 us (32%)
  blocking collectives  89.7 us (31%)
  local copies, waits for them, and re-layouts  44.8 us (16%)
  matrix products  24.2 us (8%)
  other arithmetic  16.5 us (6%)
  between operations  13.5 us (5%)
  starting transfers between devices  4.53 us (2%)
    all_to_all x1, blocking collectives, local(): lax.all_to_all(mixed, 'head', split_axis=0, concat_axis=1, tiled=True)  57.8 us
    all_gather x1, waiting for transfers between devices, local(): lax.all_gather(value_local, 'seq', axis=0, tiled=True)  55.7 us
    all_gather x1, waiting for transfers between devices, local(): lax.all_gather(key_local, 'seq', axis=0, tiled=True)  34.5 us
    all_to_all x1, blocking collectives, local(): lax.all_to_all(keys, 'head', split_axis=1, concat_axis=0, tiled=True)  19.4 us
    dot_general x8, matrix products, attend_block(): jnp.einsum('tgsd,kgd->gstk', query_block, key_all, preferred_element_type...  14.2 us
    all_to_all x1, blocking collectives, local(): lax.all_to_all(values, 'head', split_axis=1, concat_axis=0, tiled=True)  12.5 us
    dynamic_slice x16, local copies, waits for them, and re-layouts, local(): lax.map(attend_items, (query_blocks, key_blocks, value_blocks, key_far, v...  11 us
    dot_general x8, matrix products, attend_block(): jnp.einsum('gstk,kgd->tgsd', weights, value_all, preferred_element_type=j...  10 us
  transfers between devices with their start and end apart: 3, of which 2 were waited for; matrix products, arithmetic and copies ran while one was open for 6% of the time, Pallas kernels for 0%

commit v1 on v0

--- a/solution.py
+++ b/solution.py
@@ -52,7 +52,9 @@
     key_blocks = key_local.reshape(blk_dev, BS, kv_groups, width)
     value_blocks = value_local.reshape(blk_dev, BS, kv_groups, width)
     key_every, value_every = (
-        lax.all_gather(key_local, "seq", axis=0, tiled=True),
+        jnp.concatenate(
+            lax.all_to_all(jnp.stack([key_local] * lax.axis_size("seq")), "seq", 0, 0), axis=0
+        ),
         lax.all_gather(value_local, "seq", axis=0, tiled=True),
     )
     key_every = key_every.reshape(-1, BS, kv_groups, width)

time: 286 us -> 359 us (1.26)
  waiting for transfers between devices: 90.2 us -> 151 us
  starting transfers between devices: 4.53 us -> 14.9 us
  local copies, waits for them, and re-layouts: 44.8 us -> 48.5 us
    all_to_all x0 -> x1, waiting for transfers between devices: none -> 113 us  [local(): lax.all_to_all(jnp.stack([key_local] * lax.axis_size('seq')), 'seq', 0, 0)]
    all_gather x1, waiting for transfers between devices: 55.7 us -> 0.01 us  [local(): lax.all_gather(value_local, 'seq', axis=0, tiled=True)]
    all_to_all x1, waiting for transfers between devices: 0.01 us -> 37.6 us  [local(): lax.all_to_all(queries, 'head', split_axis=1, concat_axis=0, tiled=True)]
    all_gather x1 -> x0, waiting for transfers between devices: 34.5 us -> none  [local(): lax.all_gather(key_local, 'seq', axis=0, tiled=True)]
    all_to_all x0 -> x1, starting transfers between devices: none -> 10.6 us  [local(): lax.all_to_all(jnp.stack([key_local] * lax.axis_size('seq')), 'seq', 0, 0)]
    all_to_all x1, blocking collectives: 19.4 us -> 12 us  [local(): lax.all_to_all(keys, 'head', split_axis=1, concat_axis=0, tiled=True)]
    all_to_all x1, blocking collectives: 12.5 us -> 19.4 us  [local(): lax.all_to_all(values, 'head', split_axis=1, concat_axis=0, tiled=True)]
    another operation x0 -> x1, local copies, waits for them, and re-layouts: none -> 5.11 us  [local(): jnp.stack([key_local] * lax.axis_size('seq'))]
where the time goes in v1:
time: 359 us; the launch traced here: 357 us
  waiting for transfers between devices  151 us (42%)
  blocking collectives  86.6 us (24%)
  local copies, waits for them, and re-layouts  48.5 us (14%)
  matrix products  24.2 us (7%)
  other arithmetic  18.3 us (5%)
  starting transfers between devices  14.9 us (4%)
  between operations  13.5 us (4%)
    all_to_all x1, waiting for transfers between devices, local(): lax.all_to_all(jnp.stack([key_local] * lax.axis_size('seq')), 'seq', 0, 0)  113 us
    all_to_all x1, blocking collectives, local(): lax.all_to_all(mixed, 'head', split_axis=0, concat_axis=1, tiled=True)  55.1 us
    all_to_all x1, waiting for transfers between devices, local(): lax.all_to_all(queries, 'head', split_axis=1, concat_axis=0, tiled=True)  37.6 us
    all_to_all x1, blocking collectives, local(): lax.all_to_all(values, 'head', split_axis=1, concat_axis=0, tiled=True)  19.4 us
    dot_general x8, matrix products, attend_block(): jnp.einsum('tgsd,kgd->gstk', query_block, key_all, preferred_element_type...  14.2 us
    all_to_all x1, blocking collectives, local(): lax.all_to_all(keys, 'head', split_axis=1, concat_axis=0, tiled=True)  12 us
    dynamic_slice x16, local copies, waits for them, and re-layouts, local(): lax.map(attend_items, (query_blocks, key_blocks, value_blocks, key_far, v...  11.1 us
    all_to_all x1, starting transfers between devices, local(): lax.all_to_all(jnp.stack([key_local] * lax.axis_size('seq')), 'seq', 0, 0)  10.6 us
  transfers between devices with their start and end apart: 3, of which 2 were waited for; matrix products, arithmetic and copies ran while one was open for 6% of the time, Pallas kernels for 0%

profile of v1, /device:TPU:1, one launch (start us, length us, event | category | flops | bytes accessed | tf_op | source)
XLA Modules:
  0.0 357.4 jit_solution(806123503466299249)
XLA Ops:
  7.5 19.4 %all_to_all.71 = bf16[128,8,128]{2,0,1:T(8,128)(2,1)} all-to-all(bf16[128,8,128]{2,0,1:T(8,128)(2,1)S(1)} %copy.29), channel_id=1, replica_groups=mesh['seq'=32,'head'=8] {'head'}, dimensions={1} | all-to-all | bytes 524288 | tf_op jit(solution)/shard_map/all_to_all | solution.py:46
  27.9 12.0 %all_to_all.72 = bf16[128,8,128]{2,0,1:T(8,128)(2,1)S(1)} all-to-all(bf16[128,8,128]{2,0,1:T(8,128)(2,1)S(1)} %copy.30), channel_id=1, replica_groups=mesh['seq'=32,'head'=8] {'head'}, dimensions={1} | all-to-all | bytes 524288 | tf_op jit(solution)/shard_map/all_to_all | solution.py:45
  40.0 5.1 %stack.5 = bf16[32,1024,1,128]{3,1,2,0:T(8,128)(2,1)} broadcast(bf16[1024,128]{1,0:T(8,128)(2,1)S(1)} %bitcast.122), dimensions={1,3} | broadcast | bytes 8650752 | tf_op jit(solution)/shard_map/stack | solution.py:56
  45.1 10.6 %all-to-all-start.2 = ((bf16[32,1024,1,128]{3,1,2,0:T(8,128)(2,1)}), bf16[32,1024,1,128]{3,1,2,0:T(8,128)(2,1)}, u32[]{:S(2)}, u32[]{:S(2)}) async-start(bf16[32,1024,1,128]{3,1,2,0:T(8,128)(2,1)} %stack.5), calls=%async_computation.2 | async-start | bytes 16777216 | tf_op jit(solution)/shard_map/all_to_all | solution.py:56
  55.7 2.7 copy.32
  58.4 113.3 %all-to-all-done.2 = bf16[32,1024,1,128]{3,1,2,0:T(8,128)(2,1)} async-done(((bf16[32,1024,1,128]{3,1,2,0:T(8,128)(2,1)}), bf16[32,1024,1,128]{3,1,2,0:T(8,128)(2,1)}, u32[]{:S(2)}, u32[]{:S(2)}) %all-to-all-start.2) | async-done | bytes 8388640 | tf_op jit(solution)/shard_map/all_to_all | solution.py:56
  171.6 4.3 %all-to-all-start.3 = ((bf16[128,64,128]{2,0,1:T(8,128)(2,1)}), bf16[128,64,128]{2,0,1:T(8,128)(2,1)}, u32[]{:S(2)}, u32[]{:S(2)}) async-start(bf16[128,64,128]{2,0,1:T(8,128)(2,1)} %copy.32), calls=%async_computation.3 | async-start | bytes 4194304 | tf_op jit(solution)/shard_map/all_to_all | solution.py:44
  177.1 4.3 %gather_fusion.2 = bf16[64,128,128]{2,1,0:T(8,128)(2,1)S(1)} fusion(bf16[256,128,128]{2,1,0:T(8,128)(2,1)} %bitcast.29, s32[1024]{0:T(1024)S(1)} %pad_clamp_fusion), kind=kCustom, calls=%fused_computation.1.clone | custom fusion | bytes 4194560 | tf_op jit(solution)/shard_map/jit(_take)/gather | solution.py:62
  181.4 1.6 broadcast_select_fusion
  183.1 4.3 %gather_fusion.1 = bf16[64,128,128]{2,1,0:T(8,128)(2,1)S(1)} fusion(bf16[256,128,128]{2,1,0:T(8,128)(2,1)} %bitcast.126, s32[1024]{0:T(1024)S(1)} %pad_clamp_fusion), kind=kCustom, calls=%fused_computation.clone | custom fusion | bytes 4194560 | tf_op jit(solution)/shard_map/jit(_take)/gather | solution.py:63
  187.4 1.6 select_bitcast_fusion
  189.0 37.6 %all-to-all-done.3 = bf16[128,64,128]{2,0,1:T(8,128)(2,1)} async-done(((bf16[128,64,128]{2,0,1:T(8,128)(2,1)}), bf16[128,64,128]{2,0,1:T(8,128)(2,1)}, u32[]{:S(2)}, u32[]{:S(2)}) %all-to-all-start.3) | async-done | bytes 2097184 | tf_op jit(solution)/shard_map/all_to_all | solution.py:44
  226.5 67.0 %while.10 = (s32[]{:T(128)}, bf16[8,128,1,8,128]{4,3,1,0,2:T(8,128)(2,1)}, bf16[8,128,1,128]{3,1,0,2:T(8,128)(2,1)}, bf16[8,8,128,1,128]{4,2,1,3,0:T(8,128)(2,1)...) while((s32[]{:T(128)}, ...), condition=%wide.region_3.5_spmd, body=%wide.region_0.4_spmd.sunk | while | flops 616381568 | bytes 19326696 | solution.py:67
  230.1 1.8 fusion.34
  232.7 1.3 fusion.36
  238.5 1.8 fusion.34
  246.8 1.8 fusion.34
  255.2 1.8 fusion.34
  263.6 1.8 fusion.34
  271.9 1.8 fusion.34
  280.3 1.8 fusion.34
  288.7 1.8 fusion.34
  293.5 55.1 %all_to_all.73 = bf16[1024,8,128]{2,1,0:T(8,128)(2,1)S(1)} all-to-all(bf16[1024,8,128]{2,1,0:T(8,128)(2,1)} %bitcast.121), channel_id=1, replica_groups=mesh['seq'=32,'head'=8] {'head'}, dimensions={0} | all-to-all | bytes 4194304 | tf_op jit(solution)/shard_map/all_to_all | solution.py:72
  348.6 1.9 copy.42
  (138 shorter events, 54.0 us)
Async XLA Ops:
  6.5 176.5 %all-gather.2.cloned.1.call-start = ((), (), s32[]{:S(2)}) async-start(), calls=%async_computation.5 | async-start | bytes 8650752 | tf_op jit(solution)/shard_map/all_gather | solution.py:58
  45.1 10.6 %copy-start.1 = (bf16[128,64,128]{2,1,0:T(8,128)(2,1)S(1)}, bf16[128,64,128]{2,1,0:T(8,128)(2,1)}, u32[]{:S(2)}) copy-start(bf16[128,64,128]{2,1,0:T(8,128)(2,1)} %param.9) | copy-start | bytes 6291460
  45.1 126.5 %all-to-all-start.2 = ((bf16[32,1024,1,128]{3,1,2,0:T(8,128)(2,1)}), bf16[32,1024,1,128]{3,1,2,0:T(8,128)(2,1)}, u32[]{:S(2)}, u32[]{:S(2)}) async-start(bf16[32,1024,1,128]{3,1,2,0:T(8,128)(2,1)} %stack.5), calls=%async_computation.2 | async-start | bytes 16777216 | tf_op jit(solution)/shard_map/all_to_all | solution.py:56
  58.4 117.6 %copy-start.2 = (s32[8,8]{1,0:T(8,128)S(1)}, s32[8,8]{1,0:T(8,128)}, u32[]{:S(2)}) copy-start(s32[8,8]{1,0:T(8,128)} %param.12) | copy-start | bytes 772
  58.4 117.7 %copy-start = (s32[256]{0:T(256)S(1)}, s32[256]{0:T(256)}, u32[]{:S(2)}) copy-start(s32[256]{0:T(256)} %param.13) | copy-start | bytes 3076
  171.6 54.9 %all-to-all-start.3 = ((bf16[128,64,128]{2,0,1:T(8,128)(2,1)}), bf16[128,64,128]{2,0,1:T(8,128)(2,1)}, u32[]{:S(2)}, u32[]{:S(2)}) async-start(bf16[128,64,128]{2,0,1:T(8,128)(2,1)} %copy.32), calls=%async_computation.3 | async-start | bytes 4194304 | tf_op jit(solution)/shard_map/all_to_all | solution.py:44
Sparse Core Ops, SparseCore 0:
  27.1 140.8 all-gather.1

commit v2 on v0

--- a/solution.py
+++ b/solution.py
@@ -42,7 +42,10 @@
 def local(queries, keys, values, ancestors, lengths):
     query_local, key_local, value_local = (
         lax.all_to_all(queries, "head", split_axis=1, concat_axis=0, tiled=True),
-        lax.all_to_all(keys, "head", split_axis=1, concat_axis=0, tiled=True),
+        jnp.concatenate(
+            lax.all_to_all(jnp.stack(jnp.split(keys, lax.axis_size("head"), axis=1)), "head", 0, 0),
+            axis=0,
+        ),
         lax.all_to_all(values, "head", split_axis=1, concat_axis=0, tiled=True),
     )
     token_rows, head_count, width = query_local.shape

time: 286 us -> 287 us (level)
    all_gather x1, waiting for transfers between devices: 55.7 us -> 32.7 us  [local(): lax.all_gather(value_local, 'seq', axis=0, tiled=True)]
    all_gather x1, waiting for transfers between devices: 34.5 us -> 55.7 us  [local(): lax.all_gather(key_local, 'seq', axis=0, tiled=True)]
    all_to_all x1, blocking collectives: 12.5 us -> 19.4 us  [local(): lax.all_to_all(values, 'head', split_axis=1, concat_axis=0, tiled=True)]
    all_to_all x1, blocking collectives: 19.4 us -> 12.5 us  [local(): lax.all_to_all(jnp.stack(jnp.split(keys, lax.axis_size('head'), axis=1)),...]
where the time goes in v2:
time: 287 us; the launch traced here: 285 us
  blocking collectives  89.7 us (31%)
  waiting for transfers between devices  88.4 us (31%)
  local copies, waits for them, and re-layouts  47 us (16%)
  matrix products  24.2 us (8%)
  other arithmetic  17.2 us (6%)
  between operations  13.5 us (5%)
  starting transfers between devices  4.54 us (2%)
    all_to_all x1, blocking collectives, local(): lax.all_to_all(mixed, 'head', split_axis=0, concat_axis=1, tiled=True)  57.8 us
    all_gather x1, waiting for transfers between devices, local(): lax.all_gather(key_local, 'seq', axis=0, tiled=True)  55.7 us
    all_gather x1, waiting for transfers between devices, local(): lax.all_gather(value_local, 'seq', axis=0, tiled=True)  32.7 us
    all_to_all x1, blocking collectives, local(): lax.all_to_all(values, 'head', split_axis=1, concat_axis=0, tiled=True)  19.4 us
    dot_general x8, matrix products, attend_block(): jnp.einsum('tgsd,kgd->gstk', query_block, key_all, preferred_element_type...  14.2 us
    all_to_all x1, blocking collectives, local(): lax.all_to_all(jnp.stack(jnp.split(keys, lax.axis_size('head'), axis=1)),...  12.5 us
    dynamic_slice x16, local copies, waits for them, and re-layouts, local(): lax.map(attend_items, (query_blocks, key_blocks, value_blocks, key_far, v...  11.4 us
    dot_general x8, matrix products, attend_block(): jnp.einsum('gstk,kgd->tgsd', weights, value_all, preferred_element_type=j...  10 us
  transfers between devices with their start and end apart: 3, of which 2 were waited for; matrix products, arithmetic and copies ran while one was open for 6% of the time, Pallas kernels for 0%

profile of v2, /device:TPU:1, one launch (start us, length us, event | category | flops | bytes accessed | tf_op | source)
XLA Modules:
  0.0 285.3 jit_solution(1244063264035617248)
XLA Ops:
  7.7 19.4 %all_to_all.56 = bf16[128,8,128]{2,0,1:T(8,128)(2,1)} all-to-all(bf16[128,8,128]{2,0,1:T(8,128)(2,1)S(1)} %copy.48), channel_id=1, replica_groups=mesh['seq'=32,'head'=8] {'head'}, dimensions={1} | all-to-all | bytes 524288 | tf_op jit(solution)/shard_map/all_to_all | solution.py:49
  27.2 2.6 fusion.25
  30.0 12.5 %all_to_all.57 = bf16[8,128,1,128]{3,1,2,0:T(8,128)(2,1)} all-to-all(bf16[8,128,1,128]{3,1,2,0:T(8,128)(2,1)S(1)} %fusion.17), channel_id=1, replica_groups=mesh['seq'=32,'head'=8] {'head'}, dimensions={0} | all-to-all | bytes 524288 | tf_op jit(solution)/shard_map/all_to_all | solution.py:46
  42.5 2.7 copy.57
  45.2 4.5 %all-to-all-start.2 = ((bf16[128,64,128]{2,0,1:T(8,128)(2,1)}), bf16[128,64,128]{2,0,1:T(8,128)(2,1)}, u32[]{:S(2)}, u32[]{:S(2)}) async-start(bf16[128,64,128]{2,0,1:T(8,128)(2,1)} %copy.57), calls=%async_computation.2 | async-start | bytes 4194304 | tf_op jit(solution)/shard_map/all_to_all | solution.py:44
  50.8 32.7 %all-gather.3.cloned.1.call-done = bf16[32768,1,128]{2,0,1:T(8,128)(2,1)} async-done(((bf16[1024,1,128]{2,0,1:T(8,128)(2,1)}), bf16[32768,1,128]{2,0,1:T(8,128)(2,1)}) %all-gather.3.cloned.1.call-update) | async-done | bytes 8388624 | tf_op jit(solution)/shard_map/all_gather | solution.py:59
  83.5 4.3 %gather_fusion.1 = bf16[64,128,128]{2,1,0:T(8,128)(2,1)S(1)} fusion(bf16[256,128,128]{2,1,0:T(8,128)(2,1)} %bitcast.153, s32[1024]{0:T(1024)S(1)} %pad_clamp_fusion), kind=kCustom, calls=%fused_computation.clone | custom fusion | bytes 4194560 | tf_op jit(solution)/shard_map/jit(_take)/gather | solution.py:64
  87.8 55.7 %all-gather.5.cloned.1.call-done = bf16[32768,1,128]{2,0,1:T(8,128)(2,1)} async-done(((bf16[1024,1,128]{2,0,1:T(8,128)(2,1)}), bf16[32768,1,128]{2,0,1:T(8,128)(2,1)}) %all-gather.5.cloned.1.call-update) | async-done | bytes 8388624 | tf_op jit(solution)/shard_map/all_gather | solution.py:58
  143.5 5.5 %gather_fusion.2 = bf16[64,128,128]{2,1,0:T(8,128)(2,1)} fusion(bf16[256,128,128]{2,1,0:T(8,128)(2,1)} %bitcast.154, s32[1024]{0:T(1024)S(1)} %pad_clamp_fusion), kind=kCustom, calls=%fused_computation.1.clone | custom fusion | bytes 4194560 | tf_op jit(solution)/shard_map/jit(_take)/gather | solution.py:63
  149.0 1.6 select_bitcast_fusion
  151.6 67.1 %while.10 = (s32[]{:T(128)}, bf16[8,128,1,8,128]{4,3,1,0,2:T(8,128)(2,1)}, bf16[8,128,1,128]{3,1,0,2:T(8,128)(2,1)}, bf16[8,8,128,1,128]{4,2,1,3,0:T(8,128)(2,1)...) while((s32[]{:T(128)}, ...), condition=%wide.region_3.5_spmd, body=%wide.region_0.4_spmd.sunk | while | flops 616381568 | bytes 19325688 | solution.py:68
  155.2 1.8 fusion.43
  163.6 1.8 fusion.43
  172.0 1.8 fusion.43
  174.6 1.3 fusion.45
  180.4 1.8 fusion.43
  188.8 1.8 fusion.43
  191.4 1.3 fusion.45
  197.2 1.8 fusion.43
  205.5 1.8 fusion.43
  208.1 1.3 fusion.45
  213.9 1.8 fusion.43
  218.7 57.8 %all_to_all.58 = bf16[1024,8,128]{2,1,0:T(8,128)(2,1)S(1)} all-to-all(bf16[1024,8,128]{2,1,0:T(8,128)(2,1)} %bitcast.148), channel_id=1, replica_groups=mesh['seq'=32,'head'=8] {'head'}, dimensions={0} | all-to-all | bytes 4194304 | tf_op jit(solution)/shard_map/all_to_all | solution.py:73
  276.5 1.9 copy.100
  (148 shorter events, 51.9 us)
Async XLA Ops:
  6.5 36.0 %copy-start.2 = (bf16[128,64,128]{2,1,0:T(8,128)(2,1)S(1)}, bf16[128,64,128]{2,1,0:T(8,128)(2,1)}, u32[]{:S(2)}) copy-start(bf16[128,64,128]{2,1,0:T(8,128)(2,1)} %param.9) | copy-start | bytes 6291460
  6.5 76.9 %all-gather.3.cloned.1.call-start = ((), (), s32[]{:S(2)}) async-start(), calls=%async_computation.4 | async-start | bytes 8650752 | tf_op jit(solution)/shard_map/all_gather | solution.py:59
  27.1 116.4 %all-gather.5.cloned.1.call-start = ((), (), s32[]{:S(2)}) async-start(), calls=%async_computation.5 | async-start | bytes 8650752 | tf_op jit(solution)/shard_map/all_gather | solution.py:58
  45.2 4.5 %copy-start.3 = (s32[8,8]{1,0:T(8,128)S(1)}, s32[8,8]{1,0:T(8,128)}, u32[]{:S(2)}) copy-start(s32[8,8]{1,0:T(8,128)} %param.12) | copy-start | bytes 772
  45.2 4.6 %copy-start = (s32[256]{0:T(256)S(1)}, s32[256]{0:T(256)}, u32[]{:S(2)}) copy-start(s32[256]{0:T(256)} %param.13) | copy-start | bytes 3076
  45.2 106.4 %all-to-all-start.2 = ((bf16[128,64,128]{2,0,1:T(8,128)(2,1)}), bf16[128,64,128]{2,0,1:T(8,128)(2,1)}, u32[]{:S(2)}, u32[]{:S(2)}) async-start(bf16[128,64,128]{2,0,1:T(8,128)(2,1)} %copy.57), calls=%async_computation.2 | async-start | bytes 4194304 | tf_op jit(solution)/shard_map/all_to_all | solution.py:44
  149.0 2.3 copy-start.1
Sparse Core Ops, SparseCore 0:
  27.2 56.1 all-gather.2
  86.0 57.4 all-gather.4
